TPU v7x, 32 devices: a whole 2x2x4 slice. The times are simulated.
32 devices in a mesh: aa: 4 (over x, core), ba: 4 (over z), col: 2 (over y).
Axes of the slice: x: 2, y: 2, z: 4, core: 2. Of those that a mesh axis runs over, the one named last changes fastest.
Arguments:
- tokens: bfloat16 [64, 32, 64, 1024], P('aa', 'ba', 'col'), may hold values from -6 to 6
- norm_gain: float32 [1024], replicated, may hold values from 0.1 to 1.9
- in_weight: bfloat16 [1024, 3072], replicated, may hold values from -0.1875 to 0.1875
- skip_gain: float32 [1024], replicated, may hold values from 0.5 to 1.5
- spectrum_filter: bfloat16 [2, 64, 32, 64, 1024], P(None, ('ba', 'col'), None, None, 'aa'), may hold values from -4 to 4
- out_weight: bfloat16 [1024, 1024], replicated, may hold values from -0.1875 to 0.1875
Outputs:
- layer_out: bfloat16 [64, 32, 64, 1024], P('aa', 'ba', 'col')
All inputs are finite; a program needn't handle non-finite values.
Results may differ from a plain program's by a relative error of at most 0.014.
Values may be sent and summed in bfloat16 or wider, within the bound.
A program may use at most 256 MiB of HBM per device.

v0:
```python
import math
import jax
import jax.numpy as jnp
from jax import lax
from jax.sharding import PartitionSpec as P

LA = 64
LB = 32
LC = 64
D = 1024
EPSILON = 1e-06


def dft_tables(length):
    counter = jnp.arange(length, dtype=jnp.int32)
    product = counter[:, None] * counter[None, :] % length
    angle = 2.0 * math.pi / length * product.astype(jnp.float32)
    factor = 1.0 / math.sqrt(length)
    return (
        (jnp.cos(angle) * factor).astype(jnp.bfloat16),
        (jnp.sin(angle) * factor).astype(jnp.bfloat16),
    )


def phase_pair(integer_phase, modulus):
    angle = 2.0 * math.pi / modulus * (integer_phase % modulus).astype(jnp.float32)
    return (jnp.cos(angle), jnp.sin(angle))


def contract(form, table, operand):
    return jnp.einsum(form, table, operand, preferred_element_type=jnp.float32)


def local(tokens, norm_gain, in_weight, skip_gain, spectrum_filter, out_weight):
    count_aa = lax.axis_size("aa")
    count_ba = lax.axis_size("ba")
    count_col = lax.axis_size("col")
    rows_i = LA // count_aa
    rows_j = LB // count_ba
    rows_k = LC // count_col
    blocks = count_ba * count_col
    freq_local = LA // blocks
    channels = D // count_aa
    points = LA * LB * LC
    flat = tokens.reshape(-1, D).astype(jnp.float32)
    meansq = jnp.mean(flat * flat, axis=-1, keepdims=True)
    normed = (flat * lax.rsqrt(meansq + EPSILON) * norm_gain).astype(jnp.bfloat16)
    projected = jnp.dot(normed, in_weight, preferred_element_type=jnp.float32)
    mixed = (projected[:, :D] * projected[:, 2 * D :]).astype(jnp.bfloat16)
    gate = projected[:, D : 2 * D].astype(jnp.bfloat16)
    local_block = mixed.reshape(rows_i, rows_j, rows_k, D)
    by_rows = lax.all_to_all(local_block, "aa", split_axis=3, concat_axis=0, tiled=True)
    cos_a, sin_a = dft_tables(LA)
    real_part = contract("fi,ijkx->fjkx", cos_a, by_rows)
    imag_part = -contract("fi,ijkx->fjkx", sin_a, by_rows)
    j_global = lax.axis_index("ba") * rows_j + jnp.arange(rows_j, dtype=jnp.int32)
    k_global = lax.axis_index("col") * rows_k + jnp.arange(rows_k, dtype=jnp.int32)
    freq_all = jnp.arange(LA, dtype=jnp.int32)
    cos_phi, sin_phi = phase_pair(
        (LC * j_global[None, :, None] + k_global[None, None, :]) * freq_all[:, None, None], points
    )
    cos_phi = cos_phi[..., None]
    sin_phi = sin_phi[..., None]
    first = jnp.stack(
        [real_part * cos_phi + imag_part * sin_phi, imag_part * cos_phi - real_part * sin_phi]
    ).astype(jnp.bfloat16)
    shaped = first.reshape(2, blocks, 1, freq_local, rows_j, rows_k, channels)
    moved = lax.all_to_all(shaped, ("ba", "col"), split_axis=1, concat_axis=2, tiled=True)
    moved = moved.reshape(2, count_ba, count_col, freq_local, rows_j, rows_k, channels)
    cos_b, sin_b = dft_tables(LB)
    cos_b = cos_b.reshape(LB, count_ba, rows_j)
    sin_b = sin_b.reshape(LB, count_ba, rows_j)
    moved_real = moved[0]
    moved_imag = moved[1]
    form_two = "gbj,bcfjkx->fgckx"
    real_part = contract(form_two, cos_b, moved_real) + contract(form_two, sin_b, moved_imag)
    imag_part = contract(form_two, cos_b, moved_imag) - contract(form_two, sin_b, moved_real)
    index_g = jnp.arange(LB, dtype=jnp.int32)
    index_k = jnp.arange(LC, dtype=jnp.int32)
    cos_psi, sin_psi = phase_pair(index_g[:, None] * index_k[None, :], LB * LC)
    cos_psi = cos_psi.reshape(1, LB, count_col, rows_k, 1)
    sin_psi = sin_psi.reshape(1, LB, count_col, rows_k, 1)
    second_real = (real_part * cos_psi + imag_part * sin_psi).astype(jnp.bfloat16)
    second_imag = (imag_part * cos_psi - real_part * sin_psi).astype(jnp.bfloat16)
    cos_c, sin_c = dft_tables(LC)
    cos_c = cos_c.reshape(LC, count_col, rows_k)
    sin_c = sin_c.reshape(LC, count_col, rows_k)
    form_three = "hck,fgckx->fghx"
    spec_real = contract(form_three, cos_c, second_real) + contract(form_three, sin_c, second_imag)
    spec_imag = contract(form_three, cos_c, second_imag) - contract(form_three, sin_c, second_real)
    filt_real = spectrum_filter[0].astype(jnp.float32)
    filt_imag = spectrum_filter[1].astype(jnp.float32)
    filtered_real = (filt_real * spec_real - filt_imag * spec_imag).astype(jnp.bfloat16)
    filtered_imag = (filt_real * spec_imag + filt_imag * spec_real).astype(jnp.bfloat16)
    form_back_three = "hck,fghx->fgckx"
    real_part = contract(form_back_three, cos_c, filtered_real) - contract(
        form_back_three, sin_c, filtered_imag
    )
    imag_part = contract(form_back_three, cos_c, filtered_imag) + contract(
        form_back_three, sin_c, filtered_real
    )
    third_real = (real_part * cos_psi - imag_part * sin_psi).astype(jnp.bfloat16)
    third_imag = (imag_part * cos_psi + real_part * sin_psi).astype(jnp.bfloat16)
    form_back_two = "gbj,fgckx->bcfjkx"
    real_part = contract(form_back_two, cos_b, third_real) - contract(
        form_back_two, sin_b, third_imag
    )
    imag_part = contract(form_back_two, cos_b, third_imag) + contract(
        form_back_two, sin_b, third_real
    )
    slot = lax.axis_index("ba") * count_col + lax.axis_index("col")
    freq_global = slot * freq_local + jnp.arange(freq_local, dtype=jnp.int32)
    j_all = jnp.arange(LB, dtype=jnp.int32).reshape(count_ba, rows_j)
    k_all = jnp.arange(LC, dtype=jnp.int32).reshape(count_col, rows_k)
    integer_phase = (
        LC * j_all[:, None, None, :, None] + k_all[None, :, None, None, :]
    ) * freq_global[None, None, :, None, None]
    cos_back, sin_back = phase_pair(integer_phase, points)
    cos_back = cos_back[..., None]
    sin_back = sin_back[..., None]
    back_second = jnp.stack(
        [real_part * cos_back - imag_part * sin_back, imag_part * cos_back + real_part * sin_back]
    ).astype(jnp.bfloat16)
    shaped = back_second.reshape(2, 1, blocks, freq_local, rows_j, rows_k, channels)
    returned = lax.all_to_all(shaped, ("ba", "col"), split_axis=2, concat_axis=1, tiled=True)
    returned = returned.reshape(2, LA, rows_j, rows_k, channels)
    conv_part = (
        contract("fi,fjkx->ijkx", cos_a, returned[0])
        - contract("fi,fjkx->ijkx", sin_a, returned[1])
    ).astype(jnp.bfloat16)
    conv_tokens = lax.all_to_all(conv_part, "aa", split_axis=0, concat_axis=3, tiled=True)
    conv_flat = conv_tokens.reshape(-1, D).astype(jnp.float32)
    gated = (gate.astype(jnp.float32) * (conv_flat + skip_gain * mixed.astype(jnp.float32))).astype(
        jnp.bfloat16
    )
    layer_out = jnp.dot(gated, out_weight, preferred_element_type=jnp.float32).astype(jnp.bfloat16)
    return layer_out.reshape(rows_i, rows_j, rows_k, D)


def solution(mesh):
    in_specs = (
        P("aa", "ba", "col", None),
        P(),
        P(),
        P(),
        P(None, ("ba", "col"), None, None, "aa"),
        P(),
    )
    out_specs = P("aa", "ba", "col", None)
    return jax.shard_map(local, mesh=mesh, in_specs=in_specs, out_specs=out_specs, check_vma=False)
```

profile of v0, /device:TPU:0, one launch (start us, length us, event | category | flops | bytes accessed | tf_op | source)
XLA Modules:
  0.0 1626.5 jit_solution(17985871560991421885)
XLA Ops:
  10.8 31.4 %fusion.236 = f32[4096,3072]{1,0:T(8,128)} fusion(bf16[4096,1024]{1,0:T(8,128)(2,1)S(1)} %fusion.14, bf16[1024,3072]{1,0:T(8,128)(2,1)S(1)} %copy-done.8), kind=kOutput, calls=%fused_computation.280 | convolution fusion | flops 25769803776 | bytes 65011712 | tf_op jit(solution)/shard_map/dot_general | solution.py:48
  42.2 15.1 fusion.4
  57.4 44.2 %copy.74 = bf16[16,8,32,1024]{2,1,0,3:T(8,128)(2,1)} copy(bf16[16,8,32,1024]{3,2,1,0:T(8,128)(2,1)} %bitcast.244) | data formatting | bytes 16777216 | tf_op jit(solution)/shard_map/reshape | solution.py:51
  101.6 50.4 %reshape.452 = bf16[4,2,524288]{2,1,0:T(2,128)(2,1)} reshape(bf16[1024,16,8,32]{3,2,1,0:T(8,128)(2,1)} %bitcast.236) | data formatting | bytes 16777216
  159.5 92.4 %all-to-all-done = bf16[4,2,524288]{2,1,0:T(2,128)(2,1)} async-done(((bf16[4,2,524288]{2,1,0:T(2,128)(2,1)}), bf16[4,2,524288]{2,1,0:T(2,128)(2,1)}, u32[]{:S(2)}, u32[]{:S(2)}) %all-to-all-start) | async-done | bytes 8388640 | tf_op jit(solution)/shard_map/all_to_all | solution.py:52
  251.9 37.0 %reshape.453 = bf16[1024,16,8,32]{3,2,1,0:T(8,128)(2,1)} reshape(bf16[4,2,524288]{2,1,0:T(2,128)(2,1)} %all-to-all-done) | data formatting | bytes 16777216
  288.9 45.4 %copy.75 = bf16[16,8,32,4,256]{4,0,3,2,1:T(8,128)(2,1)} copy(bf16[16,8,32,4,256]{2,1,0,4,3:T(8,128)(2,1)} %bitcast.235) | data formatting | bytes 16777216 | tf_op jit(solution)/shard_map/all_to_all | solution.py:52
  351.6 11.4 copy.78
  363.0 11.4 copy.79
  374.4 13.8 pad_maximum_fusion
  399.1 358.3 %all-to-all-done.1 = bf16[2,8,1,8,8,32,256]{6,5,4,3,2,0,1:T(8,128)(2,1)} async-done(((bf16[2,8,1,8,8,32,256]{6,5,4,3,2,0,1:T(8,128)(2,1)}), bf16[2,8,1,8,8,32,256]{6,5,4,3,2,0,1:T(8,128)(2,1)}, u32[]{:S(2)}, u32[]{:S(2)}) %all-to-all-start.1) | async-done | bytes 16777248 | tf_op jit(solution)/shard_map/all_to_all | solution.py:68
  767.8 17.5 %fusion.45 = f32[2,8,32,256,32,1]{3,4,5,2,1,0:T(8,128)} fusion(bf16[4,2,8,8,32,256]{5,4,3,2,1,0:T(8,128)(2,1)} %bitcast.241, s32[4,8]{1,0:T(4,128)S(1)} %multiply_add_fusion), kind=kOutput, calls=%fused_computation.77 | convolution fusion | flops 268451840 | bytes 25165952 | tf_op jit(solution)/shard_map/gbj,bcfjkx->fgckx/dot_general | solution.py:31
  785.3 14.3 fusion.47
  808.5 26.6 %fusion.10 = (bf16[8,32,2,32,256]{4,1,3,0,2:T(8,128)(2,1)}, bf16[8,32,2,32,256]{4,1,3,0,2:T(8,128)(2,1)}) fusion(f32[32,2,32]{0,2,1:T(8,128)S(1)} %get-tuple-element.24, f32[32,2,32]{0,2,1:T(8,128)S(1)} %get-tuple-element.23, f32[2,8,32,256,32,1]{3,4,5,2,1,0:T(8,128)} %fusion.47, f32[2,8,32,256,32,1]{3,4,5,2,1,0:T(8,128)} %fusion.45, ...), kind=kOutput, calls=%fused_computation.26 | convolution fusion | flops 310394880 | bytes 75513984 | tf_op jit(solution)/shard_map/gbj,bcfjkx->fgckx/dot_general | solution.py:31
  835.2 16.0 fusion.35
  851.2 12.4 fusion.39
  863.5 21.3 %bitcast_subtract_fusion = f32[8,32,256,64]{2,3,1,0:T(8,128)} fusion(f32[8,32,256,64,1]{2,3,4,1,0:T(8,128)} %fusion.35, bf16[8,32,2,32,256]{4,1,3,0,2:T(8,128)(2,1)} %get-tuple-element.5, s32[2,32]{1,0:T(2,128)S(1)} %multiply_add_fusion.1), kind=kOutput, calls=%fused_computation.21 | convolution fusion | flops 541130752 | bytes 41943296 | tf_op jit(solution)/shard_map/hck,fgckx->fghx/dot_general | solution.py:31
  884.8 24.5 %fusion.20 = (bf16[8,32,64,256,1]{3,2,4,1,0:T(8,128)(2,1)}, bf16[8,32,64,256,1]{3,2,4,1,0:T(8,128)(2,1)S(1)}) fusion(f32[8,32,256,64]{2,3,1,0:T(8,128)} %bitcast_subtract_fusion, bf16[2,8,32,64,256]{4,3,2,1,0:T(8,128)(2,1)} %param.10, s32[2,32]{1,0:T(2,128)S(1)} %multiply_add_fusion.1, bf16[8,32,2,32,256]{4,1,3,0,2:T(8,128)(2,1)} %get-tuple-element.6, ...), kind=kOutput, calls=%fused_computation.52 | convolution fusion | flops 583073792 | bytes 75497728 | tf_op jit(solution)/shard_map/hck,fgckx->fghx/dot_general | solution.py:31
  909.3 11.7 fusion.96
  929.2 14.1 convolution_add_fusion.1
  943.3 19.4 %fusion.17 = (bf16[8,32,2,32,256,1]{4,3,2,1,0,5:T(8,128)(2,1)S(1)}, bf16[8,32,2,32,256,1]{4,3,2,1,0,5:T(8,128)(2,1)}) fusion(f32[8,32,256,2,32]{2,4,3,1,0:T(8,128)} %convolution_add_fusion.1, f32[32,2,32]{2,1,0:T(2,128)S(1)} %copy.91, f32[32,2,32]{2,1,0:T(2,128)S(1)} %copy.90, f32[8,32,256,2,32]{2,4,3,1,0:T(8,128)} %fusion.98, ...), kind=kOutput, calls=%fused_computation.49 | convolution fusion | flops 574685184 | bytes 58736896 | tf_op jit(solution)/shard_map/hck,fghx->fgckx/dot_general | solution.py:31
  973.7 14.3 fusion.29
  988.0 20.0 %convolution_subtract_fusion = f32[8,2,32,256,4,8]{3,5,4,2,1,0:T(8,128)} fusion(f32[8,2,32,256,4,8]{3,5,4,2,1,0:T(8,128)} %fusion.33, bf16[8,32,2,32,256,1]{4,3,2,1,0,5:T(8,128)(2,1)} %get-tuple-element.14, s32[4,8]{1,0:T(4,128)S(1)} %multiply_add_fusion), kind=kOutput, calls=%fused_computation.44 | convolution fusion | flops 272646144 | bytes 41943168 | tf_op jit(solution)/shard_map/gbj,fgckx->bcfjkx/dot_general | solution.py:31
  1008.0 23.1 %fusion.6 = (bf16[4,2,8,8,32,256]{5,3,0,4,1,2:T(8,128)(2,1)}, bf16[4,2,8,8,32,256]{5,3,0,4,1,2:T(8,128)(2,1)}) fusion(f32[8,2,32,256,4,8]{3,5,4,2,1,0:T(8,128)} %convolution_subtract_fusion, f32[4,2,8,8,32]{3,0,4,1,2:T(4,128)S(1)} %copy-done.6, f32[4,2,8,8,32]{3,0,4,1,2:T(4,128)S(1)} %copy-done.5, f32[8,2,32,256,4,8]{3,5,4,2,1,0:T(8,128)} %fusion.29, ...), kind=kOutput, calls=%fused_computation.16 | convolution fusion | flops 306200576 | bytes 58851456 | tf_op jit(solution)/shard_map/gbj,fgckx->bcfjkx/dot_general | solution.py:31
  1031.1 15.7 copy.98
  1046.9 15.9 copy.99
  1077.5 367.5 %all_to_all.45 = bf16[2,1,8,8,8,32,256]{6,5,4,3,1,0,2:T(8,128)(2,1)S(1)} all-to-all(bf16[2,1,8,8,8,32,256]{6,5,4,3,1,0,2:T(8,128)(2,1)} %copy.100), channel_id=1, replica_groups=mesh['aa'=4,'ba'=4,'col'=2] {'ba','col'}, dimensions={2} | all-to-all | bytes 33554432 | tf_op jit(solution)/shard_map/all_to_all | solution.py:125
  1450.0 12.5 fusion.23
  1462.5 21.2 %subtract_convert_fusion = bf16[64,8,32,256]{3,0,2,1:T(8,128)(2,1)} fusion(f32[64,8,32,256]{3,0,2,1:T(8,128)} %fusion.23, bf16[1,1,8,8,8,32,256]{6,5,4,3,1,0,2:T(8,128)(2,1)} %get-tuple-element.15), kind=kOutput, calls=%fused_computation.37 | convolution fusion | flops 545325056 | bytes 33554432 | tf_op jit(solution)/shard_map/fi,fjkx->ijkx/dot_general | solution.py:31
  1483.7 11.4 copy.103
  1495.1 97.2 %all_to_all.46 = bf16[64,8,32,256]{3,2,1,0:T(8,128)(2,1)S(1)} all-to-all(bf16[64,8,32,256]{3,2,1,0:T(8,128)(2,1)} %copy.103), channel_id=1, replica_groups=mesh['aa'=4,'ba'=4,'col'=2] {'aa'}, dimensions={0} | all-to-all | bytes 16777216 | tf_op jit(solution)/shard_map/all_to_all | solution.py:131
  1607.4 18.7 %fusion.28 = bf16[4096,1024]{1,0:T(8,128)(2,1)} fusion(bf16[1024,1024]{1,0:T(8,128)(2,1)S(1)} %copy-done, f32[4096,1024]{1,0:T(8,128)} %bitcast.250, bf16[4096,1024]{1,0:T(8,128)(2,1)S(1)} %bitcast.246, f32[4096,3072]{1,0:T(8,128)} %fusion.236, f32[1024]{0:T(1024)S(1)} %copy-done.9), kind=kOutput, calls=%fused_computation.60 | convolution fusion | flops 8619294720 | bytes 44044288 | tf_op jit(solution)/shard_map/dot_general | solution.py:136
  (57 shorter events, 119.7 us)
Async XLA Ops:
  0.0 1607.3 %copy-start = (bf16[1024,1024]{1,0:T(8,128)(2,1)S(1)}, bf16[1024,1024]{1,0:T(8,128)(2,1)}, u32[]{:S(2)}) copy-start(bf16[1024,1024]{1,0:T(8,128)(2,1)} %param.11) | copy-start | bytes 6291460
  0.0 5.4 copy-start.7
  5.4 5.4 copy-start.8
  152.0 99.9 %all-to-all-start = ((bf16[4,2,524288]{2,1,0:T(2,128)(2,1)}), bf16[4,2,524288]{2,1,0:T(2,128)(2,1)}, u32[]{:S(2)}, u32[]{:S(2)}) async-start(bf16[4,2,524288]{2,1,0:T(2,128)(2,1)} %reshape.452), calls=%async_computation | async-start | bytes 16777216 | tf_op jit(solution)/shard_map/all_to_all | solution.py:52
  334.3 6.0 copy-start.3
  388.2 369.3 %all-to-all-start.1 = ((bf16[2,8,1,8,8,32,256]{6,5,4,3,2,0,1:T(8,128)(2,1)}), bf16[2,8,1,8,8,32,256]{6,5,4,3,2,0,1:T(8,128)(2,1)}, u32[]{:S(2)}, u32[]{:S(2)}) async-start(bf16[2,8,1,8,8,32,256]{6,5,4,3,2,0,1:T(8,128)(2,1)} %pad_maximum_fusion), calls=%async_computation.1 | async-start | bytes 33554432 | tf_op jit(solution)/shard_map/all_to_all | solution.py:68
  767.8 31.8 %copy-start.4 = (bf16[1,8,1,8,8,32,256]{6,5,4,3,2,0,1:T(8,128)(2,1)}, bf16[1,8,1,8,8,32,256]{6,5,4,3,2,0,1:T(8,128)(2,1)S(1)}, u32[]{:S(2)}) copy-start(bf16[1,8,1,8,8,32,256]{6,5,4,3,2,0,1:T(8,128)(2,1)S(1)} %get-tuple-element.18) | copy-start | bytes 25165828
  835.2 16.0 copy-start.1
  962.6 11.0 copy-start.2
  988.0 20.0 %copy-start.5 = (f32[4,2,8,8,32]{3,0,4,1,2:T(4,128)S(1)}, f32[4,2,8,8,32]{3,0,4,1,2:T(4,128)}, u32[]{:S(2)}) copy-start(f32[4,2,8,8,32]{3,0,4,1,2:T(4,128)} %copy.94) | copy-start | bytes 196612
  988.0 20.0 %copy-start.6 = (f32[4,2,8,8,32]{3,0,4,1,2:T(4,128)S(1)}, f32[4,2,8,8,32]{3,0,4,1,2:T(4,128)}, u32[]{:S(2)}) copy-start(f32[4,2,8,8,32]{3,0,4,1,2:T(4,128)} %copy.97) | copy-start | bytes 196612
  1592.3 15.1 slice-start
  1599.1 8.2 slice-start.1
  1599.1 8.2 copy-start.9
where the time goes:
time: 1630 us
  blocking collectives  465 us (29%)
  waiting for transfers between devices  451 us (28%)
  matrix products  364 us (22%)
  local copies, waits for them, and re-layouts  283 us (17%)
  other arithmetic  50.3 us (3%)
    all_to_all x1, blocking collectives, local(): lax.all_to_all(shaped, ('ba', 'col'), split_axis=2, concat_axis=1, tiled=...  368 us
    all_to_all x1, waiting for transfers between devices, local(): lax.all_to_all(shaped, ('ba', 'col'), split_axis=1, concat_axis=2, tiled=...  358 us
    dot_general x20, matrix products, contract(): return jnp.einsum(form, table, operand, preferred_element_type=jnp.float32)  314 us
    all_to_all x1, blocking collectives, local(): lax.all_to_all(conv_part, 'aa', split_axis=0, concat_axis=3, tiled=True)  97.2 us
    unnamed x27, local copies, waits for them, and re-layouts  95.7 us
    all_to_all x1, waiting for transfers between devices, local(): lax.all_to_all(local_block, 'aa', split_axis=3, concat_axis=0, tiled=True)  92.4 us
    all_to_all x1, local copies, waits for them, and re-layouts, local(): lax.all_to_all(local_block, 'aa', split_axis=3, concat_axis=0, tiled=True)  45.4 us
    reshape x1, local copies, waits for them, and re-layouts, local(): local_block = mixed.reshape(rows_i, rows_j, rows_k, D)  44.2 us
  transfers between devices with their start and end apart: 2, of which 2 were waited for; matrix products, arithmetic and copies ran while one was open for 0% of the time, Pallas kernels for 0%

commit v1 on v0

--- a/solution.py
+++ b/solution.py
@@ -9,6 +9,22 @@
 LC = 64
 D = 1024
 EPSILON = 1e-06
+
+
+def exchange_in_pairs(x, axis, split, join):
+    ways, here = (lax.axis_size(axis), lax.axis_index(axis))
+    width = x.shape[split] // ways
+    dims = list(x.shape)
+    dims[split] = width
+    height = dims[join]
+    dims[join] = height * ways
+    full = jnp.zeros(dims, x.dtype)
+    for mask in range(ways):
+        part = lax.dynamic_slice_in_dim(x, (here ^ mask) * width, width, axis=split)
+        if mask:
+            part = lax.ppermute(part, axis, [(d, d ^ mask) for d in range(ways)])
+        full = lax.dynamic_update_slice_in_dim(full, part, (here ^ mask) * height, axis=join)
+    return full
 
 
 def dft_tables(length):
@@ -65,7 +81,7 @@
         [real_part * cos_phi + imag_part * sin_phi, imag_part * cos_phi - real_part * sin_phi]
     ).astype(jnp.bfloat16)
     shaped = first.reshape(2, blocks, 1, freq_local, rows_j, rows_k, channels)
-    moved = lax.all_to_all(shaped, ("ba", "col"), split_axis=1, concat_axis=2, tiled=True)
+    moved = exchange_in_pairs(shaped, ("ba", "col"), 1, 2)
     moved = moved.reshape(2, count_ba, count_col, freq_local, rows_j, rows_k, channels)
     cos_b, sin_b = dft_tables(LB)
     cos_b = cos_b.reshape(LB, count_ba, rows_j)

time: 1630 us -> 1640 us (level)
  waiting for transfers between devices: 451 us -> 340 us
  blocking collectives: 465 us -> 544 us
  local copies, waits for them, and re-layouts: 283 us -> 324 us
    all_to_all x1 -> x0, waiting for transfers between devices: 358 us -> none  [local(): lax.all_to_all(shaped, ('ba', 'col'), split_axis=1, concat_axis=2, tiled=...]
    ppermute x0 -> x7, waiting for transfers between devices: none -> 247 us  [exchange_in_pairs(): part = lax.ppermute(part, axis, [(d, d ^ mask) for d in range(ways)])]
    all_to_all x1, blocking collectives: 368 us -> 447 us  [local(): lax.all_to_all(shaped, ('ba', 'col'), split_axis=2, concat_axis=1, tiled=...]
    dynamic_update_slice x0 -> x7, local copies, waits for them, and re-layouts: none -> 21.9 us  [exchange_in_pairs(): lax.dynamic_update_slice_in_dim(full, part, (here ^ mask) * height, axis=...]
    unnamed x27 -> x36, local copies, waits for them, and re-layouts: 95.7 us -> 112 us
  transfers between devices with their start and end apart: 2 -> 8, of which waited for: 2 -> 5; matrix products, arithmetic and copies ran while one was open for 0% -> 2% of each run, Pallas kernels for 0% -> 0%
where the time goes in v1:
time: 1640 us; the launch traced here: 1630 us
  blocking collectives  544 us (33%)
  matrix products  365 us (22%)
  waiting for transfers between devices  340 us (21%)
  local copies, waits for them, and re-layouts  324 us (20%)
  other arithmetic  36.6 us (2%)
  starting transfers between devices  19.1 us (1%)
    all_to_all x1, blocking collectives, local(): lax.all_to_all(shaped, ('ba', 'col'), split_axis=2, concat_axis=1, tiled=...  447 us
    dot_general x20, matrix products, contract(): return jnp.einsum(form, table, operand, preferred_element_type=jnp.float32)  315 us
    ppermute x7, waiting for transfers between devices, exchange_in_pairs(): part = lax.ppermute(part, axis, [(d, d ^ mask) for d in range(ways)])  247 us
    unnamed x36, local copies, waits for them, and re-layouts  112 us
    all_to_all x1, blocking collectives, local(): lax.all_to_all(conv_part, 'aa', split_axis=0, concat_axis=3, tiled=True)  97.2 us
    all_to_all x1, waiting for transfers between devices, local(): lax.all_to_all(local_block, 'aa', split_axis=3, concat_axis=0, tiled=True)  92.4 us
    all_to_all x1, local copies, waits for them, and re-layouts, local(): lax.all_to_all(local_block, 'aa', split_axis=3, concat_axis=0, tiled=True)  45.4 us
    reshape x1, local copies, waits for them, and re-layouts, local(): local_block = mixed.reshape(rows_i, rows_j, rows_k, D)  44.2 us
  transfers between devices with their start and end apart: 8, of which 5 were waited for; matrix products, arithmetic and copies ran while one was open for 2% of the time, Pallas kernels for 0%

profile of v1, /device:TPU:0, one launch (start us, length us, event | category | flops | bytes accessed | tf_op | source)
XLA Modules:
  0.0 1629.3 jit_solution(16419323245428261782)
XLA Ops:
  10.8 31.4 %fusion.236 = f32[4096,3072]{1,0:T(8,128)} fusion(bf16[4096,1024]{1,0:T(8,128)(2,1)S(1)} %fusion.14, bf16[1024,3072]{1,0:T(8,128)(2,1)S(1)} %copy-done.12), kind=kOutput, calls=%fused_computation.296 | convolution fusion | flops 25769803776 | bytes 65011712 | tf_op jit(solution)/shard_map/dot_general | solution.py:64
  42.2 15.1 fusion.4
  57.4 44.2 %copy.72 = bf16[16,8,32,1024]{2,1,0,3:T(8,128)(2,1)} copy(bf16[16,8,32,1024]{3,2,1,0:T(8,128)(2,1)} %bitcast.240) | data formatting | bytes 16777216 | tf_op jit(solution)/shard_map/reshape | solution.py:67
  101.6 50.4 %reshape.446 = bf16[4,2,524288]{2,1,0:T(2,128)(2,1)} reshape(bf16[1024,16,8,32]{3,2,1,0:T(8,128)(2,1)} %bitcast.232) | data formatting | bytes 16777216
  159.5 92.4 %all-to-all-done = bf16[4,2,524288]{2,1,0:T(2,128)(2,1)} async-done(((bf16[4,2,524288]{2,1,0:T(2,128)(2,1)}), bf16[4,2,524288]{2,1,0:T(2,128)(2,1)}, u32[]{:S(2)}, u32[]{:S(2)}) %all-to-all-start) | async-done | bytes 8388640 | tf_op jit(solution)/shard_map/all_to_all | solution.py:68
  251.9 37.1 %reshape.447 = bf16[1024,16,8,32]{3,2,1,0:T(8,128)(2,1)} reshape(bf16[4,2,524288]{2,1,0:T(2,128)(2,1)} %all-to-all-done) | data formatting | bytes 16777216
  289.0 45.4 %copy.73 = bf16[16,8,32,4,256]{4,0,3,2,1:T(8,128)(2,1)} copy(bf16[16,8,32,4,256]{2,1,0,4,3:T(8,128)(2,1)} %bitcast.231) | data formatting | bytes 16777216 | tf_op jit(solution)/shard_map/all_to_all | solution.py:68
  363.1 11.5 copy_dynamic-update-slice_fusion
  399.9 39.5 %collective-permute-done = bf16[2,1,1,8,8,32,256]{6,5,4,3,2,1,0:T(8,128)(2,1)S(1)} collective-permute-done((bf16[2,1,1,8,8,32,256]{6,5,4,3,2,1,0:T(8,128)(2,1)S(1)}, bf16[2,1,1,8,8,32,256]{6,5,4,3,2,1,0:T(8,128)(2,1)S(1)}, u32[]{:S(2)}, u32[]{:S(2)}) %collective-permute-start) | collective-permute-done | bytes 2097184 | tf_op jit(solution)/shard_map/ppermute | solution.py:25
  444.5 87.2 %collective-permute-done.1 = bf16[2,1,1,8,8,32,256]{6,5,4,3,2,1,0:T(8,128)(2,1)} collective-permute-done((bf16[2,1,1,8,8,32,256]{6,5,4,3,2,1,0:T(8,128)(2,1)}, bf16[2,1,1,8,8,32,256]{6,5,4,3,2,1,0:T(8,128)(2,1)}, u32[]{:S(2)}, u32[]{:S(2)}) %collective-permute-start.1) | collective-permute-done | bytes 2097184 | tf_op jit(solution)/shard_map/ppermute | solution.py:25
  544.5 29.6 %collective-permute-done.2 = bf16[2,1,1,8,8,32,256]{6,5,4,3,2,1,0:T(8,128)(2,1)} collective-permute-done((bf16[2,1,1,8,8,32,256]{6,5,4,3,2,1,0:T(8,128)(2,1)}, bf16[2,1,1,8,8,32,256]{6,5,4,3,2,1,0:T(8,128)(2,1)}, u32[]{:S(2)}, u32[]{:S(2)}) %collective-permute-start.2) | collective-permute-done | bytes 2097184 | tf_op jit(solution)/shard_map/ppermute | solution.py:25
  580.3 91.1 %collective-permute-done.4 = bf16[2,1,1,8,8,32,256]{6,5,4,3,2,1,0:T(8,128)(2,1)} collective-permute-done((bf16[2,1,1,8,8,32,256]{6,5,4,3,2,1,0:T(8,128)(2,1)}, bf16[2,1,1,8,8,32,256]{6,5,4,3,2,1,0:T(8,128)(2,1)}, u32[]{:S(2)}, u32[]{:S(2)}) %collective-permute-start.4) | collective-permute-done | bytes 2097184 | tf_op jit(solution)/shard_map/ppermute | solution.py:25
  690.8 17.5 %fusion.45 = f32[2,8,32,256,32,1]{3,4,5,2,1,0:T(8,128)} fusion(bf16[4,2,8,8,32,256]{5,4,3,2,1,0:T(8,128)(2,1)} %bitcast.237, s32[4,8]{1,0:T(4,128)S(1)} %multiply_add_fusion), kind=kOutput, calls=%fused_computation.78 | convolution fusion | flops 268451840 | bytes 25165952 | tf_op jit(solution)/shard_map/gbj,bcfjkx->fgckx/dot_general | solution.py:47
  708.2 14.3 fusion.47
  731.6 26.7 %fusion.10 = (bf16[8,32,2,32,256]{4,1,3,0,2:T(8,128)(2,1)}, bf16[8,32,2,32,256]{4,1,3,0,2:T(8,128)(2,1)}) fusion(f32[32,2,32]{0,2,1:T(8,128)S(1)} %get-tuple-element.32, f32[32,2,32]{0,2,1:T(8,128)S(1)} %get-tuple-element.31, f32[2,8,32,256,32,1]{3,4,5,2,1,0:T(8,128)} %fusion.47, f32[2,8,32,256,32,1]{3,4,5,2,1,0:T(8,128)} %fusion.45, ...), kind=kOutput, calls=%fused_computation.25 | convolution fusion | flops 310394880 | bytes 75513984 | tf_op jit(solution)/shard_map/gbj,bcfjkx->fgckx/dot_general | solution.py:47
  758.3 16.0 fusion.35
  774.3 12.4 fusion.39
  786.6 21.3 %bitcast_subtract_fusion = f32[8,32,256,64]{2,3,1,0:T(8,128)} fusion(f32[8,32,256,64,1]{2,3,4,1,0:T(8,128)} %fusion.35, bf16[8,32,2,32,256]{4,1,3,0,2:T(8,128)(2,1)} %get-tuple-element.5, s32[2,32]{1,0:T(2,128)S(1)} %multiply_add_fusion.1), kind=kOutput, calls=%fused_computation.20 | convolution fusion | flops 541130752 | bytes 41943296 | tf_op jit(solution)/shard_map/hck,fgckx->fghx/dot_general | solution.py:47
  807.9 24.5 %fusion.20 = (bf16[8,32,64,256,1]{3,2,4,1,0:T(8,128)(2,1)}, bf16[8,32,64,256,1]{3,2,4,1,0:T(8,128)(2,1)S(1)}) fusion(f32[8,32,256,64]{2,3,1,0:T(8,128)} %bitcast_subtract_fusion, bf16[2,8,32,64,256]{4,3,2,1,0:T(8,128)(2,1)} %param.10, s32[2,32]{1,0:T(2,128)S(1)} %multiply_add_fusion.1, bf16[8,32,2,32,256]{4,1,3,0,2:T(8,128)(2,1)} %get-tuple-element.6, ...), kind=kOutput, calls=%fused_computation.51 | convolution fusion | flops 583073792 | bytes 75497728 | tf_op jit(solution)/shard_map/hck,fgckx->fghx/dot_general | solution.py:47
  832.4 11.7 fusion.96
  852.4 14.1 convolution_add_fusion.1
  866.5 19.4 %fusion.17 = (bf16[8,32,2,32,256,1]{4,3,2,1,0,5:T(8,128)(2,1)S(1)}, bf16[8,32,2,32,256,1]{4,3,2,1,0,5:T(8,128)(2,1)}) fusion(f32[8,32,256,2,32]{2,4,3,1,0:T(8,128)} %convolution_add_fusion.1, f32[32,2,32]{2,1,0:T(2,128)S(1)} %copy-done.10, f32[32,2,32]{2,1,0:T(2,128)S(1)} %copy-done.9, f32[8,32,256,2,32]{2,4,3,1,0:T(8,128)} %fusion.98, ...), kind=kOutput, calls=%fused_computation.48 | convolution fusion | flops 574685184 | bytes 58736896 | tf_op jit(solution)/shard_map/hck,fghx->fgckx/dot_general | solution.py:47
  896.9 14.3 fusion.29
  911.3 20.0 %convolution_subtract_fusion = f32[8,2,32,256,4,8]{3,5,4,2,1,0:T(8,128)} fusion(f32[8,2,32,256,4,8]{3,5,4,2,1,0:T(8,128)} %fusion.33, bf16[8,32,2,32,256,1]{4,3,2,1,0,5:T(8,128)(2,1)} %get-tuple-element.14, s32[4,8]{1,0:T(4,128)S(1)} %multiply_add_fusion), kind=kOutput, calls=%fused_computation.43 | convolution fusion | flops 272646144 | bytes 41943168 | tf_op jit(solution)/shard_map/gbj,fgckx->bcfjkx/dot_general | solution.py:47
  931.3 23.1 %fusion.6 = (bf16[4,2,8,8,32,256]{5,3,0,4,1,2:T(8,128)(2,1)}, bf16[4,2,8,8,32,256]{5,3,0,4,1,2:T(8,128)(2,1)}) fusion(f32[8,2,32,256,4,8]{3,5,4,2,1,0:T(8,128)} %convolution_subtract_fusion, f32[4,2,8,8,32]{3,0,4,1,2:T(4,128)S(1)} %copy-done.7, f32[4,2,8,8,32]{3,0,4,1,2:T(4,128)S(1)} %copy-done.6, f32[8,2,32,256,4,8]{3,5,4,2,1,0:T(8,128)} %fusion.29, ...), kind=kOutput, calls=%fused_computation.15 | convolution fusion | flops 306200576 | bytes 58851456 | tf_op jit(solution)/shard_map/gbj,fgckx->bcfjkx/dot_general | solution.py:47
  954.4 15.8 copy.94
  970.2 15.9 copy.95
  1000.9 447.0 %all_to_all.36 = bf16[2,1,8,8,8,32,256]{6,5,4,3,1,0,2:T(8,128)(2,1)S(1)} all-to-all(bf16[2,1,8,8,8,32,256]{6,5,4,3,1,0,2:T(8,128)(2,1)} %copy.96), channel_id=1, replica_groups=mesh['aa'=4,'ba'=4,'col'=2] {'ba','col'}, dimensions={2} | all-to-all | bytes 33554432 | tf_op jit(solution)/shard_map/all_to_all | solution.py:141
  1452.8 12.5 fusion.23
  1465.3 21.2 %subtract_convert_fusion = bf16[64,8,32,256]{3,0,2,1:T(8,128)(2,1)} fusion(f32[64,8,32,256]{3,0,2,1:T(8,128)} %fusion.23, bf16[1,1,8,8,8,32,256]{6,5,4,3,1,0,2:T(8,128)(2,1)} %get-tuple-element.15), kind=kOutput, calls=%fused_computation.36 | convolution fusion | flops 545325056 | bytes 33554432 | tf_op jit(solution)/shard_map/fi,fjkx->ijkx/dot_general | solution.py:47
  1497.9 97.2 %all_to_all.37 = bf16[64,8,32,256]{3,2,1,0:T(8,128)(2,1)S(1)} all-to-all(bf16[64,8,32,256]{3,2,1,0:T(8,128)(2,1)} %copy.99), channel_id=1, replica_groups=mesh['aa'=4,'ba'=4,'col'=2] {'aa'}, dimensions={0} | all-to-all | bytes 16777216 | tf_op jit(solution)/shard_map/all_to_all | solution.py:147
  1610.2 18.7 %fusion.28 = bf16[4096,1024]{1,0:T(8,128)(2,1)} fusion(bf16[1024,1024]{1,0:T(8,128)(2,1)S(1)} %copy-done, f32[4096,1024]{1,0:T(8,128)} %bitcast.246, bf16[4096,1024]{1,0:T(8,128)(2,1)S(1)} %bitcast.242, f32[4096,3072]{1,0:T(8,128)} %fusion.236, f32[1024]{0:T(1024)S(1)} %copy-done.13), kind=kOutput, calls=%fused_computation.61 | convolution fusion | flops 8619294720 | bytes 44044288 | tf_op jit(solution)/shard_map/dot_general | solution.py:152
  (85 shorter events, 190.3 us)
Async XLA Ops:
  0.0 1610.1 %copy-start = (bf16[1024,1024]{1,0:T(8,128)(2,1)S(1)}, bf16[1024,1024]{1,0:T(8,128)(2,1)}, u32[]{:S(2)}) copy-start(bf16[1024,1024]{1,0:T(8,128)(2,1)} %param.11) | copy-start | bytes 6291460
  0.0 5.4 copy-start.11
  5.4 5.4 copy-start.12
  152.0 99.9 %all-to-all-start = ((bf16[4,2,524288]{2,1,0:T(2,128)(2,1)}), bf16[4,2,524288]{2,1,0:T(2,128)(2,1)}, u32[]{:S(2)}, u32[]{:S(2)}) async-start(bf16[4,2,524288]{2,1,0:T(2,128)(2,1)} %reshape.446), calls=%async_computation | async-start | bytes 16777216 | tf_op jit(solution)/shard_map/all_to_all | solution.py:68
  334.3 6.0 copy-start.3
  374.6 11.5 copy-start.5
  391.6 47.8 %collective-permute-start = (bf16[2,1,1,8,8,32,256]{6,5,4,3,2,1,0:T(8,128)(2,1)S(1)}, bf16[2,1,1,8,8,32,256]{6,5,4,3,2,1,0:T(8,128)(2,1)S(1)}, u32[]{:S(2)}, u32[]{:S(2)}) collective-permute-start(bf16[2,1,1,8,8,32,256]{6,5,4,3,2,1,0:T(8,128)(2,1)S(1)} %get-tuple-element.25), channel_id=1, source_target_pairs={{0,1},{1,0},{2,3},{3,2},{4,5},{5,4},{6,7},{7,6},{8,9},{9,8},{10,11... | collective-permute-start | bytes 6291464 | tf_op jit(solution)/shard_map/ppermute | solution.py:25
  394.1 137.6 %collective-permute-start.1 = (bf16[2,1,1,8,8,32,256]{6,5,4,3,2,1,0:T(8,128)(2,1)}, bf16[2,1,1,8,8,32,256]{6,5,4,3,2,1,0:T(8,128)(2,1)}, u32[]{:S(2)}, u32[]{:S(2)}) collective-permute-start(bf16[2,1,1,8,8,32,256]{6,5,4,3,2,1,0:T(8,128)(2,1)} %get-tuple-element.24), channel_id=1, source_target_pairs={{0,2},{1,3},{2,0},{3,1},{4,6},{5,7},{6,4},{7,5},{8,10},{9,11},{10,... | collective-permute-start | bytes 6291464 | tf_op jit(solution)/shard_map/ppermute | solution.py:25
  395.6 178.4 %collective-permute-start.2 = (bf16[2,1,1,8,8,32,256]{6,5,4,3,2,1,0:T(8,128)(2,1)}, bf16[2,1,1,8,8,32,256]{6,5,4,3,2,1,0:T(8,128)(2,1)}, u32[]{:S(2)}, u32[]{:S(2)}) collective-permute-start(bf16[2,1,1,8,8,32,256]{6,5,4,3,2,1,0:T(8,128)(2,1)} %get-tuple-element.23), channel_id=1, source_target_pairs={{0,3},{1,2},{2,1},{3,0},{4,7},{5,6},{6,5},{7,4},{8,11},{9,10},{10,... | collective-permute-start | bytes 6291464 | tf_op jit(solution)/shard_map/ppermute | solution.py:25
  395.6 181.5 %collective-permute-start.3 = (bf16[2,1,1,8,8,32,256]{6,5,4,3,2,1,0:T(8,128)(2,1)}, bf16[2,1,1,8,8,32,256]{6,5,4,3,2,1,0:T(8,128)(2,1)}, u32[]{:S(2)}, u32[]{:S(2)}) collective-permute-start(bf16[2,1,1,8,8,32,256]{6,5,4,3,2,1,0:T(8,128)(2,1)} %get-tuple-element.22), channel_id=1, source_target_pairs={{0,4},{1,5},{2,6},{3,7},{4,0},{5,1},{6,2},{7,3},{8,12},{9,13},{10,... | collective-permute-start | bytes 6291464 | tf_op jit(solution)/shard_map/ppermute | solution.py:25
  398.6 272.8 %collective-permute-start.4 = (bf16[2,1,1,8,8,32,256]{6,5,4,3,2,1,0:T(8,128)(2,1)}, bf16[2,1,1,8,8,32,256]{6,5,4,3,2,1,0:T(8,128)(2,1)}, u32[]{:S(2)}, u32[]{:S(2)}) collective-permute-start(bf16[2,1,1,8,8,32,256]{6,5,4,3,2,1,0:T(8,128)(2,1)} %get-tuple-element.21), channel_id=1, source_target_pairs={{0,5},{1,4},{2,7},{3,6},{4,1},{5,0},{6,3},{7,2},{8,13},{9,12},{10,... | collective-permute-start | bytes 6291464 | tf_op jit(solution)/shard_map/ppermute | solution.py:25
  439.4 1.4 copy-start.8
  440.8 233.8 %collective-permute-start.5 = (bf16[2,1,1,8,8,32,256]{6,5,4,3,2,1,0:T(8,128)(2,1)}, bf16[2,1,1,8,8,32,256]{6,5,4,3,2,1,0:T(8,128)(2,1)}, u32[]{:S(2)}, u32[]{:S(2)}) collective-permute-start(bf16[2,1,1,8,8,32,256]{6,5,4,3,2,1,0:T(8,128)(2,1)} %get-tuple-element.20), channel_id=1, source_target_pairs={{0,6},{1,7},{2,4},{3,5},{4,2},{5,3},{6,0},{7,1},{8,14},{9,15},{10,... | collective-permute-start | bytes 6291464 | tf_op jit(solution)/shard_map/ppermute | solution.py:25
  531.7 145.9 %collective-permute-start.6 = (bf16[2,1,1,8,8,32,256]{6,5,4,3,2,1,0:T(8,128)(2,1)}, bf16[2,1,1,8,8,32,256]{6,5,4,3,2,1,0:T(8,128)(2,1)}, u32[]{:S(2)}, u32[]{:S(2)}) collective-permute-start(bf16[2,1,1,8,8,32,256]{6,5,4,3,2,1,0:T(8,128)(2,1)} %get-tuple-element.19), channel_id=1, source_target_pairs={{0,7},{1,6},{2,5},{3,4},{4,3},{5,2},{6,1},{7,0},{8,15},{9,14},{10,... | collective-permute-start | bytes 6291464 | tf_op jit(solution)/shard_map/ppermute | solution.py:25
  690.8 31.8 %copy-start.4 = (bf16[1,1,8,8,8,32,256]{6,5,4,3,2,1,0:T(8,128)(2,1)}, bf16[1,1,8,8,8,32,256]{6,5,4,3,2,1,0:T(8,128)(2,1)S(1)}, u32[]{:S(2)}) copy-start(bf16[1,1,8,8,8,32,256]{6,5,4,3,2,1,0:T(8,128)(2,1)S(1)} %get-tuple-element.18) | copy-start | bytes 25165828
  758.3 16.0 copy-start.1
  852.4 14.1 copy-start.9
  852.4 14.1 copy-start.10
  885.9 11.1 copy-start.2
  911.3 20.0 %copy-start.6 = (f32[4,2,8,8,32]{3,0,4,1,2:T(4,128)S(1)}, f32[4,2,8,8,32]{3,0,4,1,2:T(4,128)}, u32[]{:S(2)}) copy-start(f32[4,2,8,8,32]{3,0,4,1,2:T(4,128)} %copy.90) | copy-start | bytes 196612
  911.3 20.0 %copy-start.7 = (f32[4,2,8,8,32]{3,0,4,1,2:T(4,128)S(1)}, f32[4,2,8,8,32]{3,0,4,1,2:T(4,128)}, u32[]{:S(2)}) copy-start(f32[4,2,8,8,32]{3,0,4,1,2:T(4,128)} %copy.93) | copy-start | bytes 196612
  1595.1 15.1 slice-start
  1601.9 8.2 slice-start.1
  1602.0 8.2 copy-start.13
